TPU v7x, 512 devices: a whole 4x8x8 slice. The times are simulated.
512 devices in a mesh: dom: 64 (over x, z, core), cls: 8 (over y).
Axes of the slice: x: 4, y: 8, z: 8, core: 2. Of those that a mesh axis runs over, the one named last changes fastest.
Arguments:
- images: bfloat16 [2048, 9216], P(('dom', 'cls')), may hold values from -64 to 64
- ctf: float32 [2048, 64], P(('dom', 'cls')), may hold values from 0.2 to 1
- inv_noise: float32 [64], replicated, may hold values from 0.5 to 2
- classes: bfloat16 [400, 9216], P('cls'), may hold values from -0.25 to 0.25
- candidates: int32 [2048, 2], P(('dom', 'cls')), may hold values from 0 to 399, as said below
Outputs:
- class_sums: float32 [9216, 400], P('dom', 'cls')
- weight_sums: float32 [400, 64], P('cls')
- evidence: float32 [2048], P(('dom', 'cls'))
Inputs may be any that keep to these rules, and one draw needn't show every extreme that they name: `candidates`: each row names 2 different classes. Among the 4 particles of one device, at most 2 name a class of any one block b (classes b * 50 to (b + 1) * 50 - 1); for each index along dom, the 8 devices that share it have one common block that exactly 2 particles of each of them name.
All inputs are finite; a program needn't handle non-finite values.
Results may differ from a plain program's by a relative error of at most 0.0053.
Values may be sent and summed in bfloat16 or wider, within the bound.
No kernel may reach another device: no remote copies, remote signals or barrier semaphores. Data moves between devices by JAX's collectives and lax.ppermute only.
A program may use at most 64 MiB of HBM per device.

v0:
```python
import math
import jax
import jax.numpy as jnp
from jax import lax
from jax.sharding import PartitionSpec as P

ANGLES = 72
ROTATIONS = 36
TOP_CAND = 2
NEGATIVE = -1e30


def shards(images, ctf, inv_noise, classes, candidates):
    cls_count = lax.axis_size("cls")
    my_index = lax.axis_index("cls")
    part_dev = images.shape[0]
    class_block = classes.shape[0]
    features = images.shape[1]
    cycles = ctf.shape[1]
    capacity = min(5 * part_dev * TOP_CAND // (2 * cls_count), part_dev)
    group_size = cls_count * part_dev
    shift = features // ANGLES * (ANGLES // ROTATIONS)
    turn_ids = jnp.arange(ROTATIONS, dtype=jnp.int32)
    ctf_noise = ctf * inv_noise[None, :]
    weighted = (images.astype(jnp.float32) * jnp.tile(ctf_noise, (1, features // cycles))).astype(
        jnp.bfloat16
    )
    quadratic = (ctf * ctf * inv_noise[None, :]).astype(jnp.bfloat16)
    everyone = lax.all_gather(candidates, "cls", axis=0, tiled=True)
    block_ids = jnp.arange(class_block, dtype=jnp.int32) + my_index * class_block
    cand_mask = jnp.any(everyone[:, :, None] == block_ids[None, None, :], axis=1).astype(
        jnp.float32
    )
    owner_ids = jnp.arange(cls_count, dtype=jnp.int32)
    routed = jnp.any(
        (everyone // class_block)[:, :, None] == owner_ids[None, None, :], axis=1
    ).astype(jnp.int32)
    by_source = routed.reshape(cls_count, part_dev, cls_count)
    slot_of = jnp.cumsum(by_source, axis=1) - by_source
    slot_ids = jnp.arange(capacity, dtype=jnp.int32)
    mine_routed = lax.dynamic_index_in_dim(by_source, my_index, 0, keepdims=False)
    mine_slot = lax.dynamic_index_in_dim(slot_of, my_index, 0, keepdims=False)
    packing = (mine_routed.T[:, None, :] == 1) & (
        mine_slot.T[:, None, :] == slot_ids[None, :, None]
    )
    packing = packing.reshape(cls_count * capacity, part_dev).astype(jnp.bfloat16)
    send_data = jnp.dot(packing, weighted, preferred_element_type=jnp.float32).astype(jnp.bfloat16)
    send_quad = jnp.dot(packing, quadratic, preferred_element_type=jnp.float32).astype(jnp.bfloat16)
    row_data, row_quad = (
        lax.all_to_all(send_data, "cls", split_axis=0, concat_axis=0, tiled=True),
        lax.all_to_all(send_quad, "cls", split_axis=0, concat_axis=0, tiled=True),
    )
    into_mine = lax.dynamic_index_in_dim(by_source, my_index, 2, keepdims=False)
    slot_mine = lax.dynamic_index_in_dim(slot_of, my_index, 2, keepdims=False)
    selected = (into_mine[:, None, :] == 1) & (slot_mine[:, None, :] == slot_ids[None, :, None])
    diagonal = jnp.eye(cls_count, dtype=jnp.float32)
    unpack = (selected.astype(jnp.float32)[:, :, None, :] * diagonal[:, None, :, None]).reshape(
        cls_count * capacity, group_size
    )
    row_mask = jnp.dot(unpack, cand_mask, precision=lax.Precision.HIGHEST)
    row_count = row_data.shape[0]
    energy = jnp.sum(
        jnp.square(classes.astype(jnp.float32)).reshape(class_block, features // cycles, cycles),
        axis=1,
    )
    quad_wide = row_quad.astype(jnp.float32)
    norm_term = jnp.dot(quad_wide, energy.T, precision=lax.Precision.HIGHEST)
    twin_classes = jnp.concatenate([classes, classes], axis=1)
    feat_block = math.gcd(features, 1152)

    def add_block(block_index, running):
        offset = block_index * feat_block
        rotated = jax.vmap(
            lambda rotation: lax.dynamic_slice_in_dim(
                twin_classes, offset - rotation * shift + features, feat_block, 1
            )
        )(turn_ids)
        section = lax.dynamic_slice_in_dim(row_data, offset, feat_block, 1)
        return running + lax.dot_general(
            section, rotated, (((1,), (2,)), ((), ())), preferred_element_type=jnp.float32
        )

    cross = lax.fori_loop(
        0,
        features // feat_block,
        add_block,
        jnp.zeros((row_count, ROTATIONS, class_block), jnp.float32),
    )
    logits = cross - 0.5 * norm_term[:, None, :]
    live = jnp.broadcast_to(row_mask[:, None, :] > 0.5, logits.shape)
    masked = jnp.where(live, logits, NEGATIVE)
    peak = jnp.max(masked, axis=(1, 2))
    part_total = jnp.sum(jnp.where(live, jnp.exp(masked - peak[:, None, None]), 0.0), axis=(1, 2))
    group_peak = jnp.max(jnp.where(unpack > 0.5, peak[:, None], NEGATIVE), axis=0)
    group_total = jnp.sum(unpack * part_total[:, None], axis=0)
    back_peak, back_total = (
        lax.all_to_all(group_peak, "cls", split_axis=0, concat_axis=0, tiled=True),
        lax.all_to_all(group_total, "cls", split_axis=0, concat_axis=0, tiled=True),
    )
    back_peak = back_peak.reshape(cls_count, part_dev)
    back_total = back_total.reshape(cls_count, part_dev)
    highest = jnp.max(back_peak, axis=0)
    own_evidence = highest + jnp.log(
        jnp.sum(back_total * jnp.exp(back_peak - highest[None, :]), axis=0)
    )
    group_evidence = lax.all_gather(own_evidence, "cls", axis=0, tiled=True)
    row_evidence = jnp.dot(unpack, group_evidence, precision=lax.Precision.HIGHEST)
    posterior = jnp.where(live, jnp.exp(logits - row_evidence[:, None, None]), 0.0).astype(
        jnp.bfloat16
    )
    weight_total = jnp.sum(posterior.astype(jnp.float32), axis=1)
    ctf_part = jnp.dot(weight_total.T, quad_wide, precision=lax.Precision.HIGHEST)
    weight_sums = lax.psum(ctf_part, "dom")
    twin_rows = jnp.concatenate([row_data, row_data], axis=1)

    def add_sums(block_index, running):
        offset = block_index * feat_block
        stacked = jax.vmap(
            lambda rotation: lax.dynamic_slice_in_dim(
                twin_rows, offset + rotation * shift, feat_block, 1
            )
        )(turn_ids)
        block_sum = lax.dot_general(
            posterior, stacked, (((0, 1), (1, 0)), ((), ())), preferred_element_type=jnp.float32
        )
        return lax.dynamic_update_slice_in_dim(running, block_sum, offset, 1)

    summed = lax.fori_loop(
        0, features // feat_block, add_sums, jnp.zeros((class_block, features), jnp.float32)
    )
    full_term = summed.T
    class_sums = lax.psum_scatter(full_term, "dom", scatter_dimension=0, tiled=True)
    return (class_sums, weight_sums, own_evidence)


def solution(mesh):
    in_specs = (
        P(("dom", "cls"), None),
        P(("dom", "cls"), None),
        P(),
        P("cls", None),
        P(("dom", "cls"), None),
    )
    out_specs = (P("dom", "cls"), P("cls", None), P(("dom", "cls")))
    return jax.shard_map(shards, mesh=mesh, in_specs=in_specs, out_specs=out_specs, check_vma=False)
```

profile of v0, /device:TPU:8, one launch (start us, length us, event | category | flops | bytes accessed | tf_op | source)
XLA Modules:
  0.0 1591.2 jit_solution(15716616764184638410)
XLA Ops:
  7.2 19.5 %all-gather = s32[8,4,2]{1,2,0:T(2,128)S(1)} all-gather(s32[1,4,2]{1,2,0:T(2,128)} %bitcast.112), channel_id=1, replica_groups=mesh['dom'=64,'cls'=8] {'cls'}, dimensions={0}, use_global_device_ids=true | all-gather | bytes 288 | tf_op jit(solution)/shard_map/all_gather | solution.py:29
  28.9 3.3 all-to-all-start.1
  33.0 2.7 convert_multiply_fusion
  36.9 3.6 reshape.161
  41.4 2.3 reduce_sum.45
  43.7 7.2 all-to-all-start
  51.3 9.0 all-to-all-done
  60.4 612.1 %while.39 = (s32[]{:T(128)}, f32[16,36,50]{2,0,1:T(8,128)S(1)}, bf16[16,9216]{1,0:T(8,128)(2,1)S(1)}, bf16[50,18432]{1,0:T(8,128)(2,1)S(1)}, s32[]{:T(128)}, /*index=5*/s32[]{:T(128)}, s32[]{:T(128)}, s32[]{:T(128)}, s32[]{:T(128)}) while((s32[]{:T(128)}, f32[16,36,50]{2,0,1:T(8,128)S(1)}, bf16[16,9216]{1,0:T(8,128)(2,1)S(1)}, ...), condition=%wide.region_4.5_spmd.clone, body=%wide.region_3.4_spmd.clone.sunk | while | flops 66413024 | bytes 4840298 | solution.py:83
  60.5 71.9 %while.41 = (s32[]{:T(128)}, bf16[50,18432]{1,0:T(8,128)(2,1)S(1)}, s32[36,2]{0,1:T(2,128)S(1)}, bf16[36,50,1152]{2,1,0:T(8,128)(2,1)}, s32[]{:T(128)}) while((s32[]{:T(128)}, bf16[50,18432]{1,0:T(8,128)(2,1)S(1)}, s32[36,2]{0,1:T(2,128)S(1)}, bf16[36,50,1152]{2,1,0:T(8,128)(2,1)}, s32[]{:T(128)}) %tuple.108), condition=%wide.while_cond, body=%wide.while_body.sunk | while | flops 2 | bytes 245337 | solution.py:74
  132.3 4.6 convolution_add_fusion.2
  137.0 71.9 %while.41 = (s32[]{:T(128)}, bf16[50,18432]{1,0:T(8,128)(2,1)S(1)}, s32[36,2]{0,1:T(2,128)S(1)}, bf16[36,50,1152]{2,1,0:T(8,128)(2,1)}, s32[]{:T(128)}) while((s32[]{:T(128)}, bf16[50,18432]{1,0:T(8,128)(2,1)S(1)}, s32[36,2]{0,1:T(2,128)S(1)}, bf16[36,50,1152]{2,1,0:T(8,128)(2,1)}, s32[]{:T(128)}) %tuple.108), condition=%wide.while_cond, body=%wide.while_body.sunk | while | flops 2 | bytes 245337 | solution.py:74
  208.9 4.6 convolution_add_fusion.2
  213.5 71.9 %while.41 = (s32[]{:T(128)}, bf16[50,18432]{1,0:T(8,128)(2,1)S(1)}, s32[36,2]{0,1:T(2,128)S(1)}, bf16[36,50,1152]{2,1,0:T(8,128)(2,1)}, s32[]{:T(128)}) while((s32[]{:T(128)}, bf16[50,18432]{1,0:T(8,128)(2,1)S(1)}, s32[36,2]{0,1:T(2,128)S(1)}, bf16[36,50,1152]{2,1,0:T(8,128)(2,1)}, s32[]{:T(128)}) %tuple.108), condition=%wide.while_cond, body=%wide.while_body.sunk | while | flops 2 | bytes 245337 | solution.py:74
  285.4 4.6 convolution_add_fusion.2
  290.0 71.9 %while.41 = (s32[]{:T(128)}, bf16[50,18432]{1,0:T(8,128)(2,1)S(1)}, s32[36,2]{0,1:T(2,128)S(1)}, bf16[36,50,1152]{2,1,0:T(8,128)(2,1)}, s32[]{:T(128)}) while((s32[]{:T(128)}, bf16[50,18432]{1,0:T(8,128)(2,1)S(1)}, s32[36,2]{0,1:T(2,128)S(1)}, bf16[36,50,1152]{2,1,0:T(8,128)(2,1)}, s32[]{:T(128)}) %tuple.108), condition=%wide.while_cond, body=%wide.while_body.sunk | while | flops 2 | bytes 245337 | solution.py:74
  361.9 4.6 convolution_add_fusion.2
  366.5 71.9 %while.41 = (s32[]{:T(128)}, bf16[50,18432]{1,0:T(8,128)(2,1)S(1)}, s32[36,2]{0,1:T(2,128)S(1)}, bf16[36,50,1152]{2,1,0:T(8,128)(2,1)}, s32[]{:T(128)}) while((s32[]{:T(128)}, bf16[50,18432]{1,0:T(8,128)(2,1)S(1)}, s32[36,2]{0,1:T(2,128)S(1)}, bf16[36,50,1152]{2,1,0:T(8,128)(2,1)}, s32[]{:T(128)}) %tuple.108), condition=%wide.while_cond, body=%wide.while_body.sunk | while | flops 2 | bytes 245337 | solution.py:74
  438.4 4.6 convolution_add_fusion.2
  443.0 71.9 %while.41 = (s32[]{:T(128)}, bf16[50,18432]{1,0:T(8,128)(2,1)S(1)}, s32[36,2]{0,1:T(2,128)S(1)}, bf16[36,50,1152]{2,1,0:T(8,128)(2,1)}, s32[]{:T(128)}) while((s32[]{:T(128)}, bf16[50,18432]{1,0:T(8,128)(2,1)S(1)}, s32[36,2]{0,1:T(2,128)S(1)}, bf16[36,50,1152]{2,1,0:T(8,128)(2,1)}, s32[]{:T(128)}) %tuple.108), condition=%wide.while_cond, body=%wide.while_body.sunk | while | flops 2 | bytes 245337 | solution.py:74
  514.9 4.6 convolution_add_fusion.2
  519.5 71.9 %while.41 = (s32[]{:T(128)}, bf16[50,18432]{1,0:T(8,128)(2,1)S(1)}, s32[36,2]{0,1:T(2,128)S(1)}, bf16[36,50,1152]{2,1,0:T(8,128)(2,1)}, s32[]{:T(128)}) while((s32[]{:T(128)}, bf16[50,18432]{1,0:T(8,128)(2,1)S(1)}, s32[36,2]{0,1:T(2,128)S(1)}, bf16[36,50,1152]{2,1,0:T(8,128)(2,1)}, s32[]{:T(128)}) %tuple.108), condition=%wide.while_cond, body=%wide.while_body.sunk | while | flops 2 | bytes 245337 | solution.py:74
  591.4 4.6 convolution_add_fusion.2
  596.0 71.9 %while.41 = (s32[]{:T(128)}, bf16[50,18432]{1,0:T(8,128)(2,1)S(1)}, s32[36,2]{0,1:T(2,128)S(1)}, bf16[36,50,1152]{2,1,0:T(8,128)(2,1)}, s32[]{:T(128)}) while((s32[]{:T(128)}, bf16[50,18432]{1,0:T(8,128)(2,1)S(1)}, s32[36,2]{0,1:T(2,128)S(1)}, bf16[36,50,1152]{2,1,0:T(8,128)(2,1)}, s32[]{:T(128)}) %tuple.108), condition=%wide.while_cond, body=%wide.while_body.sunk | while | flops 2 | bytes 245337 | solution.py:74
  667.9 4.6 convolution_add_fusion.2
  673.8 4.7 all-to-all-start.3
  680.4 4.3 all-to-all-done.3
  684.7 4.7 all-to-all-start.2
  690.2 5.2 all-to-all-done.2
  696.3 15.6 all-reduce.2
  712.3 614.8 %while.37 = (s32[]{:T(128)}, f32[50,9216]{1,0:T(8,128)S(1)}, bf16[16,18432]{1,0:T(8,128)(2,1)}, bf16[16,36,50]{2,0,1:T(8,128)(2,1)S(1)}, s32[]{:T(128)}, /*index=5*/s32[]{:T(128)}, s32[]{:T(128)}, s32[]{:T(128)}, s32[]{:T(128)}) while((s32[]{:T(128)}, f32[50,9216]{1,0:T(8,128)S(1)}, bf16[16,18432]{1,0:T(8,128)(2,1)}, ...), condition=%wide.region_13.14_spmd.clone, body=%wide.region_12.13_spmd.clone.sunk | while | flops 66355388 | bytes 1807208 | solution.py:128
  712.4 76.4 %while.40 = (s32[]{:T(128)}, bf16[16,18432]{1,0:T(8,128)(2,1)}, s32[36,2]{0,1:T(2,128)S(1)}, bf16[36,16,1152]{2,1,0:T(8,128)(2,1)S(1)}, s32[]{:T(128)}) while((s32[]{:T(128)}, bf16[16,18432]{1,0:T(8,128)(2,1)}, s32[36,2]{0,1:T(2,128)S(1)}, bf16[36,16,1152]{2,1,0:T(8,128)(2,1)S(1)}, s32[]{:T(128)}) %tuple.111), condition=%wide.while_cond.1, body=%wide.while_body.1.sunk | while | flops 2 | bytes 73825 | solution.py:119
  717.3 1.5 bitcast_dynamic-update-slice_fusion.5
  725.7 1.5 bitcast_dynamic-update-slice_fusion.5
  734.2 1.5 bitcast_dynamic-update-slice_fusion.5
  757.6 1.5 bitcast_dynamic-update-slice_fusion.5
  766.1 1.5 bitcast_dynamic-update-slice_fusion.5
  774.5 1.5 bitcast_dynamic-update-slice_fusion.5
  789.3 76.4 %while.40 = (s32[]{:T(128)}, bf16[16,18432]{1,0:T(8,128)(2,1)}, s32[36,2]{0,1:T(2,128)S(1)}, bf16[36,16,1152]{2,1,0:T(8,128)(2,1)S(1)}, s32[]{:T(128)}) while((s32[]{:T(128)}, bf16[16,18432]{1,0:T(8,128)(2,1)}, s32[36,2]{0,1:T(2,128)S(1)}, bf16[36,16,1152]{2,1,0:T(8,128)(2,1)S(1)}, s32[]{:T(128)}) %tuple.111), condition=%wide.while_cond.1, body=%wide.while_body.1.sunk | while | flops 2 | bytes 73825 | solution.py:119
  789.9 1.5 bitcast_dynamic-update-slice_fusion.5
  813.2 1.5 bitcast_dynamic-update-slice_fusion.5
  821.7 1.5 bitcast_dynamic-update-slice_fusion.5
  830.2 1.5 bitcast_dynamic-update-slice_fusion.5
  853.5 1.5 bitcast_dynamic-update-slice_fusion.5
  862.0 1.5 bitcast_dynamic-update-slice_fusion.5
  866.1 76.4 %while.40 = (s32[]{:T(128)}, bf16[16,18432]{1,0:T(8,128)(2,1)}, s32[36,2]{0,1:T(2,128)S(1)}, bf16[36,16,1152]{2,1,0:T(8,128)(2,1)S(1)}, s32[]{:T(128)}) while((s32[]{:T(128)}, bf16[16,18432]{1,0:T(8,128)(2,1)}, s32[36,2]{0,1:T(2,128)S(1)}, bf16[36,16,1152]{2,1,0:T(8,128)(2,1)S(1)}, s32[]{:T(128)}) %tuple.111), condition=%wide.while_cond.1, body=%wide.while_body.1.sunk | while | flops 2 | bytes 73825 | solution.py:119
  879.4 1.5 bitcast_dynamic-update-slice_fusion.5
  887.9 1.5 bitcast_dynamic-update-slice_fusion.5
  896.4 1.5 bitcast_dynamic-update-slice_fusion.5
  919.8 1.5 bitcast_dynamic-update-slice_fusion.5
  928.2 1.5 bitcast_dynamic-update-slice_fusion.5
  936.7 1.5 bitcast_dynamic-update-slice_fusion.5
  943.0 76.4 %while.40 = (s32[]{:T(128)}, bf16[16,18432]{1,0:T(8,128)(2,1)}, s32[36,2]{0,1:T(2,128)S(1)}, bf16[36,16,1152]{2,1,0:T(8,128)(2,1)S(1)}, s32[]{:T(128)}) while((s32[]{:T(128)}, bf16[16,18432]{1,0:T(8,128)(2,1)}, s32[36,2]{0,1:T(2,128)S(1)}, bf16[36,16,1152]{2,1,0:T(8,128)(2,1)S(1)}, s32[]{:T(128)}) %tuple.111), condition=%wide.while_cond.1, body=%wide.while_body.1.sunk | while | flops 2 | bytes 73825 | solution.py:119
  945.7 1.5 bitcast_dynamic-update-slice_fusion.5
  954.2 1.5 bitcast_dynamic-update-slice_fusion.5
  962.7 1.5 bitcast_dynamic-update-slice_fusion.5
  986.0 1.5 bitcast_dynamic-update-slice_fusion.5
  994.5 1.5 bitcast_dynamic-update-slice_fusion.5
  1019.8 76.4 %while.40 = (s32[]{:T(128)}, bf16[16,18432]{1,0:T(8,128)(2,1)}, s32[36,2]{0,1:T(2,128)S(1)}, bf16[36,16,1152]{2,1,0:T(8,128)(2,1)S(1)}, s32[]{:T(128)}) while((s32[]{:T(128)}, bf16[16,18432]{1,0:T(8,128)(2,1)}, s32[36,2]{0,1:T(2,128)S(1)}, bf16[36,16,1152]{2,1,0:T(8,128)(2,1)S(1)}, s32[]{:T(128)}) %tuple.111), condition=%wide.while_cond.1, body=%wide.while_body.1.sunk | while | flops 2 | bytes 73825 | solution.py:119
  1096.7 76.4 %while.40 = (s32[]{:T(128)}, bf16[16,18432]{1,0:T(8,128)(2,1)}, s32[36,2]{0,1:T(2,128)S(1)}, bf16[36,16,1152]{2,1,0:T(8,128)(2,1)S(1)}, s32[]{:T(128)}) while((s32[]{:T(128)}, bf16[16,18432]{1,0:T(8,128)(2,1)}, s32[36,2]{0,1:T(2,128)S(1)}, bf16[36,16,1152]{2,1,0:T(8,128)(2,1)S(1)}, s32[]{:T(128)}) %tuple.111), condition=%wide.while_cond.1, body=%wide.while_body.1.sunk | while | flops 2 | bytes 73825 | solution.py:119
  1173.5 76.4 %while.40 = (s32[]{:T(128)}, bf16[16,18432]{1,0:T(8,128)(2,1)}, s32[36,2]{0,1:T(2,128)S(1)}, bf16[36,16,1152]{2,1,0:T(8,128)(2,1)S(1)}, s32[]{:T(128)}) while((s32[]{:T(128)}, bf16[16,18432]{1,0:T(8,128)(2,1)}, s32[36,2]{0,1:T(2,128)S(1)}, bf16[36,16,1152]{2,1,0:T(8,128)(2,1)S(1)}, s32[]{:T(128)}) %tuple.111), condition=%wide.while_cond.1, body=%wide.while_body.1.sunk | while | flops 2 | bytes 73825 | solution.py:119
  1250.4 76.4 %while.40 = (s32[]{:T(128)}, bf16[16,18432]{1,0:T(8,128)(2,1)}, s32[36,2]{0,1:T(2,128)S(1)}, bf16[36,16,1152]{2,1,0:T(8,128)(2,1)S(1)}, s32[]{:T(128)}) while((s32[]{:T(128)}, bf16[16,18432]{1,0:T(8,128)(2,1)}, s32[36,2]{0,1:T(2,128)S(1)}, bf16[36,16,1152]{2,1,0:T(8,128)(2,1)S(1)}, s32[]{:T(128)}) %tuple.111), condition=%wide.while_cond.1, body=%wide.while_body.1.sunk | while | flops 2 | bytes 73825 | solution.py:119
  1327.2 3.4 copy.77
  1330.8 251.9 %psum.7 = f32[50,64]{1,0:T(8,128)} all-reduce(f32[50,64]{1,0:T(8,128)S(1)} %fusion.19), channel_id=1, replica_groups=mesh['dom'=64,'cls'=8] {'dom'}, use_global_device_ids=true, to_apply=%region_16.17 | all-reduce | flops 3200 | bytes 25600 | tf_op jit(solution)/shard_map/psum | solution.py:113
  1582.8 1.6 copy.78
  (1827 shorter events, 1159.5 us)
Async XLA Ops:
  7.2 28.5 %copy-start = (bf16[50,9216]{1,0:T(8,128)(2,1)S(1)}, bf16[50,9216]{1,0:T(8,128)(2,1)}, u32[]{:S(2)}) copy-start(bf16[50,9216]{1,0:T(8,128)(2,1)} %param.12) | copy-start | bytes 2764804
  28.9 14.8 all-to-all-start.1
  35.6 0.9 copy-start.1
  43.7 16.6 %all-to-all-start = ((bf16[8,2,9216]{2,1,0:T(2,128)(2,1)}), bf16[8,2,9216]{2,1,0:T(2,128)(2,1)S(1)}, u32[]{:S(2)}, u32[]{:S(2)}) async-start(bf16[8,2,9216]{2,1,0:T(2,128)(2,1)} %all_to_all.28), calls=%async_computation | async-start | bytes 589824 | tf_op jit(solution)/shard_map/all_to_all | solution.py:50
  673.8 10.8 all-to-all-start.3
  684.7 10.8 all-to-all-start.2
  689.3 893.4 %reduce-scatter.4.cloned.1.call-start = ((), (), s32[]{:S(2)}) async-start(), calls=%async_computation.5 | async-start | bytes 4792320
Sparse Core Ops, SparseCore 0:
  1330.7 154.5 reduce-scatter.3
where the time goes:
time: 1620 us; the launch traced here: 1590 us
  local copies, waits for them, and re-layouts  1190 us (73%)
  blocking collectives  287 us (18%)
  matrix products  42.2 us (3%)
  starting transfers between devices  19.9 us (1%)
  waiting for transfers between devices  18.6 us (1%)
    gather x1728, local copies, waits for them, and re-layouts  1180 us
    psum x1, blocking collectives, shards(): weight_sums = lax.psum(ctf_part, 'dom')  252 us
    dot_general x8, matrix products, add_block(): lax.dot_general(section, rotated, (((1,), (2,)), ((), ())), preferred_ele...  36.8 us
  transfers between devices with their start and end apart: 5, of which 3 were waited for; matrix products, arithmetic and copies ran while one was open for 1% of the time, Pallas kernels for 0%

commit v1 on v0

--- a/solution.py
+++ b/solution.py
@@ -110,7 +110,7 @@
     )
     weight_total = jnp.sum(posterior.astype(jnp.float32), axis=1)
     ctf_part = jnp.dot(weight_total.T, quad_wide, precision=lax.Precision.HIGHEST)
-    weight_sums = lax.psum(ctf_part, "dom")
+    weight_sums = jnp.sum(lax.all_gather(ctf_part, "dom"), axis=0)
     twin_rows = jnp.concatenate([row_data, row_data], axis=1)
 
     def add_sums(block_index, running):

time: 1620 us -> 1520 us (0.938)
  blocking collectives: 287 us -> 91 us
  waiting for transfers between devices: 18.6 us -> 116 us
    psum x1 -> x0, blocking collectives: 252 us -> none  [shards(): weight_sums = lax.psum(ctf_part, 'dom')]
    unnamed x2, waiting for transfers between devices: 0.02 us -> 97.8 us
    all_gather x0 -> x1, blocking collectives: none -> 56 us  [shards(): weight_sums = jnp.sum(lax.all_gather(ctf_part, 'dom'), axis=0)]
  transfers between devices with their start and end apart: 5 -> 5, of which waited for: 3 -> 4; matrix products, arithmetic and copies ran while one was open for 1% -> 1% of each run, Pallas kernels for 0% -> 0%
where the time goes in v1:
time: 1520 us; the launch traced here: 1490 us
  local copies, waits for them, and re-layouts  1190 us (78%)
  waiting for transfers between devices  116 us (8%)
  blocking collectives  91 us (6%)
  matrix products  42.2 us (3%)
  starting transfers between devices  19.9 us (1%)
    gather x1728, local copies, waits for them, and re-layouts  1180 us
    unnamed x2, waiting for transfers between devices  97.8 us
    all_gather x1, blocking collectives, shards(): weight_sums = jnp.sum(lax.all_gather(ctf_part, 'dom'), axis=0)  56 us
    dot_general x8, matrix products, add_block(): lax.dot_general(section, rotated, (((1,), (2,)), ((), ())), preferred_ele...  36.8 us
  transfers between devices with their start and end apart: 5, of which 4 were waited for; matrix products, arithmetic and copies ran while one was open for 1% of the time, Pallas kernels for 0%

profile of v1, /device:TPU:8, one launch (start us, length us, event | category | flops | bytes accessed | tf_op | source)
XLA Modules:
  0.0 1493.8 jit_solution(5663281973816775624)
XLA Ops:
  7.2 19.5 %all-gather.1 = s32[8,4,2]{1,2,0:T(2,128)S(1)} all-gather(s32[1,4,2]{1,2,0:T(2,128)} %bitcast.114), channel_id=1, replica_groups=mesh['dom'=64,'cls'=8] {'cls'}, dimensions={0}, use_global_device_ids=true | all-gather | bytes 288 | tf_op jit(solution)/shard_map/all_gather | solution.py:29
  28.9 3.3 all-to-all-start.1
  33.0 2.7 convert_multiply_fusion
  36.9 3.6 reshape.161
  41.4 2.3 reduce_sum.54
  43.7 7.2 all-to-all-start
  51.3 9.0 all-to-all-done
  60.4 612.1 %while.39 = (s32[]{:T(128)}, f32[16,36,50]{2,0,1:T(8,128)S(1)}, bf16[16,9216]{1,0:T(8,128)(2,1)S(1)}, bf16[50,18432]{1,0:T(8,128)(2,1)S(1)}, s32[]{:T(128)}, /*index=5*/s32[]{:T(128)}, s32[]{:T(128)}, s32[]{:T(128)}, s32[]{:T(128)}) while((s32[]{:T(128)}, f32[16,36,50]{2,0,1:T(8,128)S(1)}, bf16[16,9216]{1,0:T(8,128)(2,1)S(1)}, ...), condition=%wide.region_4.5_spmd.clone, body=%wide.region_3.4_spmd.clone.sunk | while | flops 66413024 | bytes 4840298 | solution.py:83
  60.5 71.9 %while.41 = (s32[]{:T(128)}, bf16[50,18432]{1,0:T(8,128)(2,1)S(1)}, s32[36,2]{0,1:T(2,128)S(1)}, bf16[36,50,1152]{2,1,0:T(8,128)(2,1)}, s32[]{:T(128)}) while((s32[]{:T(128)}, bf16[50,18432]{1,0:T(8,128)(2,1)S(1)}, s32[36,2]{0,1:T(2,128)S(1)}, bf16[36,50,1152]{2,1,0:T(8,128)(2,1)}, s32[]{:T(128)}) %tuple.108), condition=%wide.while_cond, body=%wide.while_body.sunk | while | flops 2 | bytes 245337 | solution.py:74
  132.3 4.6 convolution_add_fusion.2
  137.0 71.9 %while.41 = (s32[]{:T(128)}, bf16[50,18432]{1,0:T(8,128)(2,1)S(1)}, s32[36,2]{0,1:T(2,128)S(1)}, bf16[36,50,1152]{2,1,0:T(8,128)(2,1)}, s32[]{:T(128)}) while((s32[]{:T(128)}, bf16[50,18432]{1,0:T(8,128)(2,1)S(1)}, s32[36,2]{0,1:T(2,128)S(1)}, bf16[36,50,1152]{2,1,0:T(8,128)(2,1)}, s32[]{:T(128)}) %tuple.108), condition=%wide.while_cond, body=%wide.while_body.sunk | while | flops 2 | bytes 245337 | solution.py:74
  208.9 4.6 convolution_add_fusion.2
  213.5 71.9 %while.41 = (s32[]{:T(128)}, bf16[50,18432]{1,0:T(8,128)(2,1)S(1)}, s32[36,2]{0,1:T(2,128)S(1)}, bf16[36,50,1152]{2,1,0:T(8,128)(2,1)}, s32[]{:T(128)}) while((s32[]{:T(128)}, bf16[50,18432]{1,0:T(8,128)(2,1)S(1)}, s32[36,2]{0,1:T(2,128)S(1)}, bf16[36,50,1152]{2,1,0:T(8,128)(2,1)}, s32[]{:T(128)}) %tuple.108), condition=%wide.while_cond, body=%wide.while_body.sunk | while | flops 2 | bytes 245337 | solution.py:74
  285.4 4.6 convolution_add_fusion.2
  290.0 71.9 %while.41 = (s32[]{:T(128)}, bf16[50,18432]{1,0:T(8,128)(2,1)S(1)}, s32[36,2]{0,1:T(2,128)S(1)}, bf16[36,50,1152]{2,1,0:T(8,128)(2,1)}, s32[]{:T(128)}) while((s32[]{:T(128)}, bf16[50,18432]{1,0:T(8,128)(2,1)S(1)}, s32[36,2]{0,1:T(2,128)S(1)}, bf16[36,50,1152]{2,1,0:T(8,128)(2,1)}, s32[]{:T(128)}) %tuple.108), condition=%wide.while_cond, body=%wide.while_body.sunk | while | flops 2 | bytes 245337 | solution.py:74
  361.9 4.6 convolution_add_fusion.2
  366.5 71.9 %while.41 = (s32[]{:T(128)}, bf16[50,18432]{1,0:T(8,128)(2,1)S(1)}, s32[36,2]{0,1:T(2,128)S(1)}, bf16[36,50,1152]{2,1,0:T(8,128)(2,1)}, s32[]{:T(128)}) while((s32[]{:T(128)}, bf16[50,18432]{1,0:T(8,128)(2,1)S(1)}, s32[36,2]{0,1:T(2,128)S(1)}, bf16[36,50,1152]{2,1,0:T(8,128)(2,1)}, s32[]{:T(128)}) %tuple.108), condition=%wide.while_cond, body=%wide.while_body.sunk | while | flops 2 | bytes 245337 | solution.py:74
  438.4 4.6 convolution_add_fusion.2
  443.0 71.9 %while.41 = (s32[]{:T(128)}, bf16[50,18432]{1,0:T(8,128)(2,1)S(1)}, s32[36,2]{0,1:T(2,128)S(1)}, bf16[36,50,1152]{2,1,0:T(8,128)(2,1)}, s32[]{:T(128)}) while((s32[]{:T(128)}, bf16[50,18432]{1,0:T(8,128)(2,1)S(1)}, s32[36,2]{0,1:T(2,128)S(1)}, bf16[36,50,1152]{2,1,0:T(8,128)(2,1)}, s32[]{:T(128)}) %tuple.108), condition=%wide.while_cond, body=%wide.while_body.sunk | while | flops 2 | bytes 245337 | solution.py:74
  514.9 4.6 convolution_add_fusion.2
  519.5 71.9 %while.41 = (s32[]{:T(128)}, bf16[50,18432]{1,0:T(8,128)(2,1)S(1)}, s32[36,2]{0,1:T(2,128)S(1)}, bf16[36,50,1152]{2,1,0:T(8,128)(2,1)}, s32[]{:T(128)}) while((s32[]{:T(128)}, bf16[50,18432]{1,0:T(8,128)(2,1)S(1)}, s32[36,2]{0,1:T(2,128)S(1)}, bf16[36,50,1152]{2,1,0:T(8,128)(2,1)}, s32[]{:T(128)}) %tuple.108), condition=%wide.while_cond, body=%wide.while_body.sunk | while | flops 2 | bytes 245337 | solution.py:74
  591.4 4.6 convolution_add_fusion.2
  596.0 71.9 %while.41 = (s32[]{:T(128)}, bf16[50,18432]{1,0:T(8,128)(2,1)S(1)}, s32[36,2]{0,1:T(2,128)S(1)}, bf16[36,50,1152]{2,1,0:T(8,128)(2,1)}, s32[]{:T(128)}) while((s32[]{:T(128)}, bf16[50,18432]{1,0:T(8,128)(2,1)S(1)}, s32[36,2]{0,1:T(2,128)S(1)}, bf16[36,50,1152]{2,1,0:T(8,128)(2,1)}, s32[]{:T(128)}) %tuple.108), condition=%wide.while_cond, body=%wide.while_body.sunk | while | flops 2 | bytes 245337 | solution.py:74
  667.9 4.6 convolution_add_fusion.2
  673.8 4.7 all-to-all-start.3
  680.4 4.3 all-to-all-done.3
  684.7 4.7 all-to-all-start.2
  690.2 5.2 all-to-all-done.2
  696.3 15.6 %all-reduce.2 = f32[32]{0:T(128)S(1)} all-reduce(f32[32]{0:T(128)S(1)} %get-tuple-element.320), channel_id=1, replica_groups=mesh['dom'=64,'cls'=8] {'cls'}, use_global_device_ids=true, to_apply=%add.2 | all-reduce | flops 32 | bytes 256
  712.3 614.8 %while.37 = (s32[]{:T(128)}, f32[50,9216]{1,0:T(8,128)S(1)}, bf16[16,18432]{1,0:T(8,128)(2,1)}, bf16[16,36,50]{2,0,1:T(8,128)(2,1)S(1)}, s32[]{:T(128)}, /*index=5*/s32[]{:T(128)}, s32[]{:T(128)}, s32[]{:T(128)}, s32[]{:T(128)}) while((s32[]{:T(128)}, f32[50,9216]{1,0:T(8,128)S(1)}, bf16[16,18432]{1,0:T(8,128)(2,1)}, ...), condition=%wide.region_13.14_spmd.clone, body=%wide.region_12.13_spmd.clone.sunk | while | flops 66355388 | bytes 1807208 | solution.py:128
  712.4 76.4 %while.40 = (s32[]{:T(128)}, bf16[16,18432]{1,0:T(8,128)(2,1)}, s32[36,2]{0,1:T(2,128)S(1)}, bf16[36,16,1152]{2,1,0:T(8,128)(2,1)S(1)}, s32[]{:T(128)}) while((s32[]{:T(128)}, bf16[16,18432]{1,0:T(8,128)(2,1)}, s32[36,2]{0,1:T(2,128)S(1)}, bf16[36,16,1152]{2,1,0:T(8,128)(2,1)S(1)}, s32[]{:T(128)}) %tuple.111), condition=%wide.while_cond.1, body=%wide.while_body.1.sunk | while | flops 2 | bytes 73825 | solution.py:119
  717.3 1.5 bitcast_dynamic-update-slice_fusion.5
  725.7 1.5 bitcast_dynamic-update-slice_fusion.5
  734.2 1.5 bitcast_dynamic-update-slice_fusion.5
  757.6 1.5 bitcast_dynamic-update-slice_fusion.5
  766.1 1.5 bitcast_dynamic-update-slice_fusion.5
  774.5 1.5 bitcast_dynamic-update-slice_fusion.5
  789.3 76.4 %while.40 = (s32[]{:T(128)}, bf16[16,18432]{1,0:T(8,128)(2,1)}, s32[36,2]{0,1:T(2,128)S(1)}, bf16[36,16,1152]{2,1,0:T(8,128)(2,1)S(1)}, s32[]{:T(128)}) while((s32[]{:T(128)}, bf16[16,18432]{1,0:T(8,128)(2,1)}, s32[36,2]{0,1:T(2,128)S(1)}, bf16[36,16,1152]{2,1,0:T(8,128)(2,1)S(1)}, s32[]{:T(128)}) %tuple.111), condition=%wide.while_cond.1, body=%wide.while_body.1.sunk | while | flops 2 | bytes 73825 | solution.py:119
  789.9 1.5 bitcast_dynamic-update-slice_fusion.5
  813.2 1.5 bitcast_dynamic-update-slice_fusion.5
  821.7 1.5 bitcast_dynamic-update-slice_fusion.5
  830.2 1.5 bitcast_dynamic-update-slice_fusion.5
  853.5 1.5 bitcast_dynamic-update-slice_fusion.5
  862.0 1.5 bitcast_dynamic-update-slice_fusion.5
  866.1 76.4 %while.40 = (s32[]{:T(128)}, bf16[16,18432]{1,0:T(8,128)(2,1)}, s32[36,2]{0,1:T(2,128)S(1)}, bf16[36,16,1152]{2,1,0:T(8,128)(2,1)S(1)}, s32[]{:T(128)}) while((s32[]{:T(128)}, bf16[16,18432]{1,0:T(8,128)(2,1)}, s32[36,2]{0,1:T(2,128)S(1)}, bf16[36,16,1152]{2,1,0:T(8,128)(2,1)S(1)}, s32[]{:T(128)}) %tuple.111), condition=%wide.while_cond.1, body=%wide.while_body.1.sunk | while | flops 2 | bytes 73825 | solution.py:119
  879.4 1.5 bitcast_dynamic-update-slice_fusion.5
  887.9 1.5 bitcast_dynamic-update-slice_fusion.5
  896.4 1.5 bitcast_dynamic-update-slice_fusion.5
  919.8 1.5 bitcast_dynamic-update-slice_fusion.5
  928.2 1.5 bitcast_dynamic-update-slice_fusion.5
  936.7 1.5 bitcast_dynamic-update-slice_fusion.5
  943.0 76.4 %while.40 = (s32[]{:T(128)}, bf16[16,18432]{1,0:T(8,128)(2,1)}, s32[36,2]{0,1:T(2,128)S(1)}, bf16[36,16,1152]{2,1,0:T(8,128)(2,1)S(1)}, s32[]{:T(128)}) while((s32[]{:T(128)}, bf16[16,18432]{1,0:T(8,128)(2,1)}, s32[36,2]{0,1:T(2,128)S(1)}, bf16[36,16,1152]{2,1,0:T(8,128)(2,1)S(1)}, s32[]{:T(128)}) %tuple.111), condition=%wide.while_cond.1, body=%wide.while_body.1.sunk | while | flops 2 | bytes 73825 | solution.py:119
  945.7 1.5 bitcast_dynamic-update-slice_fusion.5
  954.2 1.5 bitcast_dynamic-update-slice_fusion.5
  962.7 1.5 bitcast_dynamic-update-slice_fusion.5
  986.0 1.5 bitcast_dynamic-update-slice_fusion.5
  1019.8 76.4 %while.40 = (s32[]{:T(128)}, bf16[16,18432]{1,0:T(8,128)(2,1)}, s32[36,2]{0,1:T(2,128)S(1)}, bf16[36,16,1152]{2,1,0:T(8,128)(2,1)S(1)}, s32[]{:T(128)}) while((s32[]{:T(128)}, bf16[16,18432]{1,0:T(8,128)(2,1)}, s32[36,2]{0,1:T(2,128)S(1)}, bf16[36,16,1152]{2,1,0:T(8,128)(2,1)S(1)}, s32[]{:T(128)}) %tuple.111), condition=%wide.while_cond.1, body=%wide.while_body.1.sunk | while | flops 2 | bytes 73825 | solution.py:119
  1096.7 76.4 %while.40 = (s32[]{:T(128)}, bf16[16,18432]{1,0:T(8,128)(2,1)}, s32[36,2]{0,1:T(2,128)S(1)}, bf16[36,16,1152]{2,1,0:T(8,128)(2,1)S(1)}, s32[]{:T(128)}) while((s32[]{:T(128)}, bf16[16,18432]{1,0:T(8,128)(2,1)}, s32[36,2]{0,1:T(2,128)S(1)}, bf16[36,16,1152]{2,1,0:T(8,128)(2,1)S(1)}, s32[]{:T(128)}) %tuple.111), condition=%wide.while_cond.1, body=%wide.while_body.1.sunk | while | flops 2 | bytes 73825 | solution.py:119
  1173.5 76.4 %while.40 = (s32[]{:T(128)}, bf16[16,18432]{1,0:T(8,128)(2,1)}, s32[36,2]{0,1:T(2,128)S(1)}, bf16[36,16,1152]{2,1,0:T(8,128)(2,1)S(1)}, s32[]{:T(128)}) while((s32[]{:T(128)}, bf16[16,18432]{1,0:T(8,128)(2,1)}, s32[36,2]{0,1:T(2,128)S(1)}, bf16[36,16,1152]{2,1,0:T(8,128)(2,1)S(1)}, s32[]{:T(128)}) %tuple.111), condition=%wide.while_cond.1, body=%wide.while_body.1.sunk | while | flops 2 | bytes 73825 | solution.py:119
  1250.4 76.4 %while.40 = (s32[]{:T(128)}, bf16[16,18432]{1,0:T(8,128)(2,1)}, s32[36,2]{0,1:T(2,128)S(1)}, bf16[36,16,1152]{2,1,0:T(8,128)(2,1)S(1)}, s32[]{:T(128)}) while((s32[]{:T(128)}, bf16[16,18432]{1,0:T(8,128)(2,1)}, s32[36,2]{0,1:T(2,128)S(1)}, bf16[36,16,1152]{2,1,0:T(8,128)(2,1)S(1)}, s32[]{:T(128)}) %tuple.111), condition=%wide.while_cond.1, body=%wide.while_body.1.sunk | while | flops 2 | bytes 73825 | solution.py:119
  1327.2 3.4 copy.77
  1330.8 56.0 %all-gather.2 = f32[64,50,64]{2,1,0:T(8,128)S(1)} all-gather(f32[1,50,64]{2,1,0:T(8,128)S(1)} %convolution_bitcast_fusion.1), channel_id=2, replica_groups=mesh['dom'=64,'cls'=8] {'dom'}, dimensions={0}, use_global_device_ids=true | all-gather | bytes 832000 | tf_op jit(solution)/shard_map/all_gather | solution.py:113
  1387.6 97.8 %reduce-scatter.4.cloned.1.call-done = f32[144,50]{1,0:T(8,128)} async-done(((f32[9216,50]{1,0:T(8,128)}), f32[144,50]{1,0:T(8,128)}) %reduce-scatter.4.cloned.1.call-update) | async-done | bytes 28816
  1485.4 1.6 copy.78
  (1828 shorter events, 1161.8 us)
Async XLA Ops:
  7.2 28.5 %copy-start = (bf16[50,9216]{1,0:T(8,128)(2,1)S(1)}, bf16[50,9216]{1,0:T(8,128)(2,1)}, u32[]{:S(2)}) copy-start(bf16[50,9216]{1,0:T(8,128)(2,1)} %param.12) | copy-start | bytes 2764804
  28.9 14.8 all-to-all-start.1
  35.6 0.9 copy-start.1
  43.7 16.6 %all-to-all-start = ((bf16[8,2,9216]{2,1,0:T(2,128)(2,1)}), bf16[8,2,9216]{2,1,0:T(2,128)(2,1)S(1)}, u32[]{:S(2)}, u32[]{:S(2)}) async-start(bf16[8,2,9216]{2,1,0:T(2,128)(2,1)} %all_to_all.28), calls=%async_computation | async-start | bytes 589824 | tf_op jit(solution)/shard_map/all_to_all | solution.py:50
  673.8 10.8 all-to-all-start.3
  684.7 10.8 all-to-all-start.2
  689.3 796.1 %reduce-scatter.4.cloned.1.call-start = ((), (), s32[]{:S(2)}) async-start(), calls=%async_computation.5 | async-start | bytes 4792320
Sparse Core Ops, SparseCore 0:
  1330.7 154.5 reduce-scatter.3
